TPU v7x, 512 devices: a whole 4x4x16 slice. The times are simulated.
512 devices in a mesh: row: 128 (over y, z, core), col: 4 (over x).
Axes of the slice: x: 4, y: 4, z: 16, core: 2. Of those that a mesh axis runs over, the one named last changes fastest.
Arguments:
- residual: float32 [65536, 128], P('row'), may hold values from -6 to 6
- solution: float32 [65536, 128], P('row'), may hold values from -6 to 6
- near_field_blocks: float32 [256, 4, 256, 256], P('row', 'col'), may hold values from -0.09375 to 0.09375
- near_cols: int32 [256, 4], P('row', 'col'), may hold values from 0 to 255, as said below
- couplings: float32 [256, 64, 16, 16], P('row', 'col'), may hold values from -0.1875 to 0.1875
- far_cols: int32 [256, 64], P('row', 'col'), may hold values from 0 to 255, as said below
- far_count: int32 [256], P('row'), may hold values from 16 to 64, as said below
- col_basis: float32 [256, 16, 256], P('row'), may hold values from -0.375 to 0.375
- row_basis: float32 [256, 16, 256], P('row'), may hold values from -0.75 to 0.75
Outputs:
- solution_next: float32 [65536, 128], P('row')
- hessenberg: float32 [5, 4, 128], replicated
Inputs may be any that keep to these rules, and one draw needn't show every extreme that they name: near_cols[i, 0] = i; the other entries of row cluster i are i + t for distinct nonzero t with |t| <= 2, clipped to 0 .. 255. far_cols[i, p] differs from i by more than 2, counted around the ends of the cluster range. Slots p >= far_count[i] of row cluster i are unused; some row cluster uses all 64 slots.
All inputs are finite; a program needn't handle non-finite values.
Results may differ from a plain program's by a relative error of at most 0.0001.
Values sent between devices are 32-bit elements; how exact they have to be, the bound alone decides.
A program may use at most 64 MiB of HBM per device.

v0:
```python
import jax
import jax.numpy as jnp
from jax import lax
from jax.sharding import PartitionSpec as P

LEAF_UNKNOWNS = 256
CL_DEV = 2
REACH = 2
SB = 4
HIGH = lax.Precision.HIGHEST
SHIFT = 1.0


def with_halo(value, sides, width):
    for axis, dim in sides:
        peers, length = (lax.axis_size(axis), value.shape[dim])
        up = [(i, (i + 1) % peers) for i in range(peers - 1)]
        down = [(j, i) for i, j in up]
        last = lax.slice_in_dim(value, length - width, length, axis=dim)
        first = lax.slice_in_dim(value, 0, width, axis=dim)
        before = lax.ppermute(last, axis, up)
        after = lax.ppermute(first, axis, down)
        value = jnp.concatenate([before, value, after], axis=dim)
    return value


def cholesky_upper(entries, order_n):
    zero_entry = jnp.zeros_like(entries[0][0])
    upper_r = []
    for row_idx in range(order_n):
        upper_r.append([zero_entry] * order_n)
    for row_idx in range(order_n):
        running = entries[row_idx][row_idx]
        for earlier in range(row_idx):
            running = running - upper_r[earlier][row_idx] * upper_r[earlier][row_idx]
        pivot_val = jnp.sqrt(running)
        upper_r[row_idx][row_idx] = pivot_val
        for col_idx in range(row_idx + 1, order_n):
            entry_val = entries[row_idx][col_idx]
            for earlier in range(row_idx):
                entry_val = entry_val - upper_r[earlier][row_idx] * upper_r[earlier][col_idx]
            upper_r[row_idx][col_idx] = entry_val / pivot_val
    return upper_r


def small_update(gram_sum, scale_factor, depth_n):
    order_n = depth_n + 1
    entries = [
        [gram_sum[row_idx, col_idx] for col_idx in range(order_n)] for row_idx in range(order_n)
    ]
    upper_r = cholesky_upper(entries, order_n)
    shifted = [
        [
            SHIFT * upper_r[row_idx][col_idx] + upper_r[row_idx][col_idx + 1]
            for col_idx in range(depth_n)
        ]
        for row_idx in range(order_n)
    ]
    hessen = []
    for row_idx in range(order_n):
        row_vals = []
        for col_idx in range(depth_n):
            entry_val = shifted[row_idx][col_idx]
            for earlier in range(col_idx):
                entry_val = entry_val - row_vals[earlier] * upper_r[earlier][col_idx]
            row_vals.append(entry_val / upper_r[col_idx][col_idx])
        hessen.append(row_vals)
    normal = []
    for row_idx in range(depth_n):
        row_vals = []
        for col_idx in range(depth_n):
            entry_val = hessen[0][row_idx] * hessen[0][col_idx]
            for inner in range(1, order_n):
                entry_val = entry_val + hessen[inner][row_idx] * hessen[inner][col_idx]
            row_vals.append(entry_val)
        normal.append(row_vals)
    target = [scale_factor * upper_r[0][0] * hessen[0][col_idx] for col_idx in range(depth_n)]
    factor = cholesky_upper(normal, depth_n)
    forward = []
    for row_idx in range(depth_n):
        entry_val = target[row_idx]
        for earlier in range(row_idx):
            entry_val = entry_val - factor[earlier][row_idx] * forward[earlier]
        forward.append(entry_val / factor[row_idx][row_idx])
    solved = [None] * depth_n
    for row_idx in range(depth_n - 1, -1, -1):
        entry_val = forward[row_idx]
        for later in range(row_idx + 1, depth_n):
            entry_val = entry_val - factor[row_idx][later] * solved[later]
        solved[row_idx] = entry_val / factor[row_idx][row_idx]
    weights = [None] * depth_n
    for row_idx in range(depth_n - 1, -1, -1):
        entry_val = solved[row_idx]
        for later in range(row_idx + 1, depth_n):
            entry_val = entry_val - upper_r[row_idx][later] * weights[later]
        weights[row_idx] = entry_val / upper_r[row_idx][row_idx]
    hess_array = jnp.stack([jnp.stack(hessen[row_idx], 0) for row_idx in range(order_n)], 0)
    return (hess_array, weights)


def local(
    residual,
    solution,
    near_field_blocks,
    near_cols,
    couplings,
    far_cols,
    far_count,
    col_basis,
    row_basis,
):
    first_cluster = lax.axis_index("row") * CL_DEV
    blocks, couple = (near_field_blocks, couplings)
    near_idx, far_idx = (near_cols, far_cols)
    positions = lax.axis_index("col") * couplings.shape[1] + jnp.arange(
        couplings.shape[1], dtype=jnp.int32
    )
    live_mask = (positions[None, :] < far_count[:, None]).astype(jnp.float32)
    weighted = couple * live_mask[:, :, None, None]
    local_near = near_idx - (first_cluster - REACH)
    scale_factor = jnp.ones((residual.shape[1],), jnp.float32)
    current = residual
    basis_list = [current]
    for step_k in range(SB):
        width_r = current.shape[1]
        extended = with_halo(current, (("row", 0),), REACH * LEAF_UNKNOWNS)
        panels = extended.reshape(CL_DEV + 2 * REACH, LEAF_UNKNOWNS, width_r)
        picked = jnp.take(panels, local_near, axis=0)
        near_part = jnp.einsum("csab,csbr->car", blocks, picked, precision=HIGH)
        own_panels = current.reshape(CL_DEV, LEAF_UNKNOWNS, width_r)
        coeffs = jnp.einsum("ckb,cbr->ckr", col_basis, own_panels, precision=HIGH)
        table = lax.all_gather(coeffs, "row", axis=0, tiled=True)
        fetched = jnp.take(table, far_idx, axis=0)
        summed = jnp.einsum("cfkl,cflr->ckr", weighted, fetched, precision=HIGH)
        far_part = jnp.einsum("ckb,ckr->cbr", row_basis, summed, precision=HIGH)
        partial_value = (near_part + far_part).reshape(CL_DEV * LEAF_UNKNOWNS, width_r)
        current = lax.psum(partial_value, "col")
        basis_list.append(current)
    stacked = jnp.stack(basis_list, 0)
    local_gram = jnp.einsum("anr,bnr->abr", stacked, stacked, precision=HIGH)
    gram_sum = lax.psum(local_gram, "row")
    hessenberg, weights = small_update(gram_sum, scale_factor, SB)
    new_sol = solution
    for step_k in range(SB):
        new_sol = new_sol + weights[step_k][None, :] * basis_list[step_k]
    return (new_sol, hessenberg)


def solution(mesh):
    placed = (
        P("row", None),
        P("row", None),
        P("row", "col", None, None),
        P("row", "col"),
        P("row", "col", None, None),
        P("row", "col"),
        P("row"),
        P("row", None, None),
        P("row", None, None),
    )
    return jax.shard_map(
        local, mesh=mesh, in_specs=placed, out_specs=(P("row", None), P()), check_vma=False
    )
```

profile of v0, /device:TPU:4, one launch (start us, length us, event | category | flops | bytes accessed | tf_op | source)
XLA Modules:
  0.0 1346.1 jit_solution(8567163214037070050)
XLA Ops:
  7.2 1.9 fusion.85
  9.2 1.8 collective-permute-start
  11.0 1.3 collective-permute-start.1
  14.5 1.8 collective-permute-done.1
  17.9 139.1 %all-gather.5.cloned.1.call-done = f32[256,16,128]{2,1,0:T(8,128)} async-done(((f32[2,16,128]{2,1,0:T(8,128)}), f32[256,16,128]{2,1,0:T(8,128)}) %all-gather.5.cloned.1.call-update) | async-done | bytes 2097168 | tf_op jit(solution)/shard_map/all_gather | solution.py:132
  157.0 2.2 gather_fusion.1
  162.2 52.8 %all-reduce.5.cloned.1.call-done = f32[512,128]{0,1:T(8,128)} async-done(((f32[512,128]{0,1:T(8,128)}), f32[512,128]{0,1:T(8,128)}) %all-reduce.5.cloned.1.call-update) | async-done | bytes 262160 | tf_op jit(solution)/shard_map/psum | solution.py:137
  215.1 1.1 copy.50
  217.1 1.3 collective-permute-start.2
  218.4 1.3 collective-permute-start.3
  219.7 4.1 collective-permute-done.3
  225.7 135.3 %all-gather.7.cloned.1.call-done = f32[256,16,128]{2,1,0:T(8,128)} async-done(((f32[2,16,128]{2,1,0:T(8,128)}), f32[256,16,128]{2,1,0:T(8,128)}) %all-gather.7.cloned.1.call-update) | async-done | bytes 2097168 | tf_op jit(solution)/shard_map/all_gather | solution.py:132
  360.9 2.2 gather_fusion.3
  366.2 52.8 %all-reduce.7.cloned.1.call-done = f32[512,128]{0,1:T(8,128)} async-done(((f32[512,128]{0,1:T(8,128)}), f32[512,128]{0,1:T(8,128)}) %all-reduce.7.cloned.1.call-update) | async-done | bytes 262160 | tf_op jit(solution)/shard_map/psum | solution.py:137
  419.0 1.1 copy.55
  421.0 1.3 collective-permute-start.4
  422.3 1.3 collective-permute-start.5
  423.6 4.1 collective-permute-done.5
  429.6 135.1 %all-gather.9.cloned.1.call-done = f32[256,16,128]{2,1,0:T(8,128)} async-done(((f32[2,16,128]{2,1,0:T(8,128)}), f32[256,16,128]{2,1,0:T(8,128)}) %all-gather.9.cloned.1.call-update) | async-done | bytes 2097168 | tf_op jit(solution)/shard_map/all_gather | solution.py:132
  564.7 2.2 gather_fusion.5
  569.9 52.8 %all-reduce.9.cloned.1.call-done = f32[512,128]{0,1:T(8,128)} async-done(((f32[512,128]{0,1:T(8,128)}), f32[512,128]{0,1:T(8,128)}) %all-reduce.9.cloned.1.call-update) | async-done | bytes 262160 | tf_op jit(solution)/shard_map/psum | solution.py:137
  622.7 1.1 copy.60
  624.8 1.3 collective-permute-start.6
  626.1 1.5 collective-permute-start.7
  627.6 3.9 collective-permute-done.7
  633.4 135.3 %all-gather.11.cloned.1.call-done = f32[256,16,128]{2,1,0:T(8,128)} async-done(((f32[2,16,128]{2,1,0:T(8,128)}), f32[256,16,128]{2,1,0:T(8,128)}) %all-gather.11.cloned.1.call-update) | async-done | bytes 2097168 | tf_op jit(solution)/shard_map/all_gather | solution.py:132
  768.6 2.2 gather_fusion.7
  779.2 47.4 %all-reduce.11.cloned.1.call-done = f32[1,512,128]{1,0,2:T(1,128)} async-done(((f32[1,512,128]{1,0,2:T(1,128)}), f32[1,512,128]{1,0,2:T(1,128)}) %all-reduce.11.cloned.1.call-update) | async-done | bytes 262160 | tf_op jit(solution)/shard_map/psum | solution.py:137
  826.6 4.6 stack.76
  831.2 3.7 convolution_bitcast_fusion
  834.9 495.3 %psum.39 = f32[5,5,128]{0,1,2:T(8,128)S(1)} all-reduce(f32[5,5,128]{0,1,2:T(8,128)} %convolution_bitcast_fusion), channel_id=1, replica_groups=mesh['row'=128,'col'=4] {'row'}, use_global_device_ids=true, to_apply=%region_4.7 | all-reduce | flops 3200 | bytes 25600 | tf_op jit(solution)/shard_map/psum | solution.py:141
  1330.2 6.9 multiply_reduce_fusion
  (107 shorter events, 31.7 us)
Async XLA Ops:
  7.2 153.2 %copy-start = (f32[2,1,256,256]{3,2,1,0:T(8,128)S(1)}, f32[2,1,256,256]{3,2,1,0:T(8,128)}, u32[]{:S(2)}) copy-start(f32[2,1,256,256]{3,2,1,0:T(8,128)} %param.15) | copy-start | bytes 1572868
  7.2 152.0 %copy-start.1 = (f32[2,16,16,16]{3,2,1,0:T(8,128)S(1)}, f32[2,16,16,16]{3,2,1,0:T(8,128)}, u32[]{:S(2)}) copy-start(f32[2,16,16,16]{3,2,1,0:T(8,128)} %param.17) | copy-start | bytes 98308
  7.2 152.7 %copy-start.9 = (f32[2,16,256]{2,1,0:T(8,128)S(1)}, f32[2,16,256]{2,1,0:T(8,128)}, u32[]{:S(2)}) copy-start(f32[2,16,256]{2,1,0:T(8,128)} %param.21) | copy-start | bytes 98308
  7.2 149.8 %all-gather.5.cloned.1.call-start = ((), (), s32[]{:S(2)}) async-start(), calls=%async_computation | async-start | bytes 2113536 | tf_op jit(solution)/shard_map/all_gather | solution.py:132
  9.2 205.9 %all-reduce.5.cloned.1.call-start = ((), (), s32[]{:S(2)}) async-start(), calls=%async_computation.1 | async-start | bytes 524288 | tf_op jit(solution)/shard_map/psum | solution.py:137
  9.2 5.3 collective-permute-start
  11.0 5.3 collective-permute-start.1
  159.1 57.0 %copy-start.8 = (f32[2,16,256]{2,1,0:T(8,128)S(1)}, f32[2,16,256]{2,1,0:T(8,128)}, u32[]{:S(2)}) copy-start(f32[2,16,256]{2,1,0:T(8,128)} %param.20) | copy-start | bytes 98308
  162.2 198.8 %all-gather.7.cloned.1.call-start = ((), (), s32[]{:S(2)}) async-start(), calls=%async_computation.2 | async-start | bytes 2113536 | tf_op jit(solution)/shard_map/all_gather | solution.py:132
  217.0 201.9 %all-reduce.7.cloned.1.call-start = ((), (), s32[]{:S(2)}) async-start(), calls=%async_computation.3 | async-start | bytes 524288 | tf_op jit(solution)/shard_map/psum | solution.py:137
  217.1 2.7 collective-permute-start.2
  218.4 5.4 collective-permute-start.3
  366.1 198.6 %all-gather.9.cloned.1.call-start = ((), (), s32[]{:S(2)}) async-start(), calls=%async_computation.4 | async-start | bytes 2113536 | tf_op jit(solution)/shard_map/all_gather | solution.py:132
  420.9 201.8 %all-reduce.9.cloned.1.call-start = ((), (), s32[]{:S(2)}) async-start(), calls=%async_computation.5 | async-start | bytes 524288 | tf_op jit(solution)/shard_map/psum | solution.py:137
  421.0 2.7 collective-permute-start.4
  422.3 5.4 collective-permute-start.5
  569.9 198.7 %all-gather.11.cloned.1.call-start = ((), (), s32[]{:S(2)}) async-start(), calls=%async_computation.6 | async-start | bytes 2113536 | tf_op jit(solution)/shard_map/all_gather | solution.py:132
  624.7 201.9 %all-reduce.11.cloned.1.call-start = ((), (), s32[]{:S(2)}) async-start(), calls=%async_computation.7 | async-start | bytes 524288 | tf_op jit(solution)/shard_map/psum | solution.py:137
  624.8 2.8 collective-permute-start.6
  626.1 5.4 collective-permute-start.7
  633.3 140.5 %copy-start.2 = (f32[512,128]{1,0:T(8,128)S(1)}, f32[512,128]{1,0:T(8,128)}, u32[]{:S(2)}) copy-start(f32[512,128]{1,0:T(8,128)} %param.13) | copy-start | bytes 786436
  771.6 3.9 copy-start.10
  772.0 4.3 copy-start.3
  772.0 5.3 copy-start.4
  772.8 5.5 copy-start.5
  834.9 502.6 %copy-start.6 = (f32[512,128]{0,1:T(8,128)S(1)}, f32[512,128]{0,1:T(8,128)}, u32[]{:S(2)}) copy-start(f32[512,128]{0,1:T(8,128)} %copy.65) | copy-start | bytes 786436
  834.9 502.6 %copy-start.7 = (f32[512,128]{0,1:T(8,128)S(1)}, f32[512,128]{0,1:T(8,128)}, u32[]{:S(2)}) copy-start(f32[512,128]{0,1:T(8,128)} %copy.66) | copy-start | bytes 786436
  1338.6 0.6 copy-start.11
Sparse Core Ops, SparseCore 0:
  11.7 145.1 all-gather.4
  162.3 52.7 all-reduce.4
  218.8 142.1 all-gather.6
  366.2 52.6 all-reduce.6
  422.5 142.1 all-gather.8
  570.0 52.7 all-reduce.8
  626.5 142.1 all-gather.10
  773.9 52.6 all-reduce.10
where the time goes:
time: 1350 us
  waiting for transfers between devices  765 us (57%)
  blocking collectives  495 us (37%)
  local copies, waits for them, and re-layouts  30.2 us (2%)
  matrix products  16.2 us (1%)
  between operations  14.7 us (1%)
  other arithmetic  13.6 us (1%)
    all_gather x4, waiting for transfers between devices, local(): table = lax.all_gather(coeffs, 'row', axis=0, tiled=True)  545 us
    psum x1, blocking collectives, local(): gram_sum = lax.psum(local_gram, 'row')  495 us
    psum x4, waiting for transfers between devices, local(): current = lax.psum(partial_value, 'col')  206 us
  transfers between devices with their start and end apart: 16, of which 12 were waited for; matrix products, arithmetic and copies ran while one was open for 1% of the time, Pallas kernels for 0%

commit v1 on v0

--- a/solution.py
+++ b/solution.py
@@ -129,7 +129,17 @@
         near_part = jnp.einsum("csab,csbr->car", blocks, picked, precision=HIGH)
         own_panels = current.reshape(CL_DEV, LEAF_UNKNOWNS, width_r)
         coeffs = jnp.einsum("ckb,cbr->ckr", col_basis, own_panels, precision=HIGH)
-        table = lax.all_gather(coeffs, "row", axis=0, tiled=True)
+
+        def compute_classes(original):
+            right_arr = lax.all_to_all(
+                jnp.stack(lax.psum(1, axis_name="row") * [original]),
+                axis_name="row",
+                split_axis=0,
+                concat_axis=0,
+            )
+            return jnp.concatenate(right_arr, axis=0)
+
+        table = compute_classes(coeffs)
         fetched = jnp.take(table, far_idx, axis=0)
         summed = jnp.einsum("cfkl,cflr->ckr", weighted, fetched, precision=HIGH)
         far_part = jnp.einsum("ckb,ckr->cbr", row_basis, summed, precision=HIGH)

time: 1350 us -> 1240 us (0.919)
  waiting for transfers between devices: 765 us -> 584 us
  starting transfers between devices: 11.3 us -> 84.7 us
    all_gather x4 -> x0, waiting for transfers between devices: 545 us -> none  [local(): table = lax.all_gather(coeffs, 'row', axis=0, tiled=True)]
    all_to_all x0 -> x4, waiting for transfers between devices: none -> 366 us  [compute_classes(): lax.all_to_all(jnp.stack(lax.psum(1, axis_name='row') * [original]), axis...]
    all_to_all x0 -> x4, starting transfers between devices: none -> 73.2 us  [compute_classes(): lax.all_to_all(jnp.stack(lax.psum(1, axis_name='row') * [original]), axis...]
where the time goes in v1:
time: 1240 us
  waiting for transfers between devices  584 us (47%)
  blocking collectives  496 us (40%)
  starting transfers between devices  84.7 us (7%)
  local copies, waits for them, and re-layouts  36.4 us (3%)
  between operations  14.4 us (1%)
  matrix products  13.7 us (1%)
    psum x1, blocking collectives, local(): gram_sum = lax.psum(local_gram, 'row')  496 us
    all_to_all x4, waiting for transfers between devices, compute_classes(): lax.all_to_all(jnp.stack(lax.psum(1, axis_name='row') * [original]), axis...  366 us
    psum x4, waiting for transfers between devices, local(): current = lax.psum(partial_value, 'col')  205 us
    all_to_all x4, starting transfers between devices, compute_classes(): lax.all_to_all(jnp.stack(lax.psum(1, axis_name='row') * [original]), axis...  73.2 us
  transfers between devices with their start and end apart: 16, of which 12 were waited for; matrix products, arithmetic and copies ran while one was open for 1% of the time, Pallas kernels for 0%

profile of v1, /device:TPU:4, one launch (start us, length us, event | category | flops | bytes accessed | tf_op | source)
XLA Modules:
  0.0 1236.4 jit_solution(1824168152202112509)
XLA Ops:
  8.4 1.6 stack.43
  10.0 20.6 %all-to-all-start = ((f32[128,2,16,128]{3,2,1,0:T(8,128)}), f32[128,2,16,128]{3,2,1,0:T(8,128)}, u32[]{:S(2)}, u32[]{:S(2)}) async-start(f32[128,2,16,128]{3,2,1,0:T(8,128)} %stack.43), calls=%async_computation | async-start | bytes 4194304 | tf_op jit(solution)/shard_map/all_to_all | solution.py:134
  30.7 1.6 collective-permute-start
  33.9 3.0 collective-permute-done.1
  37.5 91.6 %all-to-all-done = f32[128,2,16,128]{3,2,1,0:T(8,128)} async-done(((f32[128,2,16,128]{3,2,1,0:T(8,128)}), f32[128,2,16,128]{3,2,1,0:T(8,128)}, u32[]{:S(2)}, u32[]{:S(2)}) %all-to-all-start) | async-done | bytes 2097184 | tf_op jit(solution)/shard_map/all_to_all | solution.py:134
  129.1 2.2 gather_fusion.1
  134.3 52.5 %all-reduce.5.cloned.1.call-done = f32[512,128]{0,1:T(8,128)} async-done(((f32[512,128]{0,1:T(8,128)}), f32[512,128]{0,1:T(8,128)}) %all-reduce.5.cloned.1.call-update) | async-done | bytes 262160 | tf_op jit(solution)/shard_map/psum | solution.py:147
  188.1 1.6 stack.45
  189.7 17.5 %all-to-all-start.1 = ((f32[128,2,16,128]{3,2,1,0:T(8,128)}), f32[128,2,16,128]{3,2,1,0:T(8,128)}, u32[]{:S(2)}, u32[]{:S(2)}) async-start(f32[128,2,16,128]{3,2,1,0:T(8,128)} %stack.45), calls=%async_computation.1 | async-start | bytes 4194304 | tf_op jit(solution)/shard_map/all_to_all | solution.py:134
  207.3 1.5 collective-permute-start.2
  210.1 3.2 collective-permute-done.3
  214.2 91.4 %all-to-all-done.1 = f32[128,2,16,128]{3,2,1,0:T(8,128)} async-done(((f32[128,2,16,128]{3,2,1,0:T(8,128)}), f32[128,2,16,128]{3,2,1,0:T(8,128)}, u32[]{:S(2)}, u32[]{:S(2)}) %all-to-all-start.1) | async-done | bytes 2097184 | tf_op jit(solution)/shard_map/all_to_all | solution.py:134
  305.6 2.2 gather_fusion.3
  310.8 52.7 %all-reduce.7.cloned.1.call-done = f32[512,128]{0,1:T(8,128)} async-done(((f32[512,128]{0,1:T(8,128)}), f32[512,128]{0,1:T(8,128)}) %all-reduce.7.cloned.1.call-update) | async-done | bytes 262160 | tf_op jit(solution)/shard_map/psum | solution.py:147
  364.9 1.6 stack.47
  366.5 17.5 %all-to-all-start.2 = ((f32[128,2,16,128]{3,2,1,0:T(8,128)}), f32[128,2,16,128]{3,2,1,0:T(8,128)}, u32[]{:S(2)}, u32[]{:S(2)}) async-start(f32[128,2,16,128]{3,2,1,0:T(8,128)} %stack.47), calls=%async_computation.2 | async-start | bytes 4194304 | tf_op jit(solution)/shard_map/all_to_all | solution.py:134
  385.5 1.5 collective-permute-start.5
  387.0 3.1 collective-permute-done.5
  391.0 91.4 %all-to-all-done.2 = f32[128,2,16,128]{3,2,1,0:T(8,128)} async-done(((f32[128,2,16,128]{3,2,1,0:T(8,128)}), f32[128,2,16,128]{3,2,1,0:T(8,128)}, u32[]{:S(2)}, u32[]{:S(2)}) %all-to-all-start.2) | async-done | bytes 2097184 | tf_op jit(solution)/shard_map/all_to_all | solution.py:134
  482.4 2.2 gather_fusion.5
  487.6 52.7 %all-reduce.9.cloned.1.call-done = f32[512,128]{0,1:T(8,128)} async-done(((f32[512,128]{0,1:T(8,128)}), f32[512,128]{0,1:T(8,128)}) %all-reduce.9.cloned.1.call-update) | async-done | bytes 262160 | tf_op jit(solution)/shard_map/psum | solution.py:147
  541.7 1.6 stack.49
  543.3 17.5 %all-to-all-start.3 = ((f32[128,2,16,128]{3,2,1,0:T(8,128)}), f32[128,2,16,128]{3,2,1,0:T(8,128)}, u32[]{:S(2)}, u32[]{:S(2)}) async-start(f32[128,2,16,128]{3,2,1,0:T(8,128)} %stack.49), calls=%async_computation.3 | async-start | bytes 4194304 | tf_op jit(solution)/shard_map/all_to_all | solution.py:134
  560.8 1.5 collective-permute-start.6
  563.6 3.2 collective-permute-done.7
  567.8 91.4 %all-to-all-done.3 = f32[128,2,16,128]{3,2,1,0:T(8,128)} async-done(((f32[128,2,16,128]{3,2,1,0:T(8,128)}), f32[128,2,16,128]{3,2,1,0:T(8,128)}, u32[]{:S(2)}, u32[]{:S(2)}) %all-to-all-start.3) | async-done | bytes 2097184 | tf_op jit(solution)/shard_map/all_to_all | solution.py:134
  659.2 2.2 gather_fusion.7
  669.8 47.4 %all-reduce.11.cloned.1.call-done = f32[1,512,128]{1,0,2:T(1,128)} async-done(((f32[1,512,128]{1,0,2:T(1,128)}), f32[1,512,128]{1,0,2:T(1,128)}) %all-reduce.11.cloned.1.call-update) | async-done | bytes 262160 | tf_op jit(solution)/shard_map/psum | solution.py:147
  717.1 4.5 stack.51
  721.6 3.7 convolution_bitcast_fusion
  725.3 495.5 %psum.39 = f32[5,5,128]{0,1,2:T(8,128)S(1)} all-reduce(f32[5,5,128]{0,1,2:T(8,128)} %convolution_bitcast_fusion), channel_id=1, replica_groups=mesh['row'=128,'col'=4] {'row'}, use_global_device_ids=true, to_apply=%region_4.7 | all-reduce | flops 3200 | bytes 25600 | tf_op jit(solution)/shard_map/psum | solution.py:151
  1220.9 6.9 multiply_reduce_fusion
  (117 shorter events, 33.5 us)
Async XLA Ops:
  7.2 125.3 %copy-start = (f32[2,1,256,256]{3,2,1,0:T(8,128)S(1)}, f32[2,1,256,256]{3,2,1,0:T(8,128)}, u32[]{:S(2)}) copy-start(f32[2,1,256,256]{3,2,1,0:T(8,128)} %param.15) | copy-start | bytes 1572868
  10.0 20.7 %copy-start.2 = (f32[512,128]{1,0:T(8,128)S(1)}, f32[512,128]{1,0:T(8,128)}, u32[]{:S(2)}) copy-start(f32[512,128]{1,0:T(8,128)} %param.13) | copy-start | bytes 786436
  10.0 23.6 %copy-start.13 = (s32[2,16]{1,0:T(2,128)S(1)}, s32[2,16]{1,0:T(2,128)}, u32[]{:S(2)}) copy-start(s32[2,16]{1,0:T(2,128)} %param.18) | copy-start | bytes 388
  10.0 23.7 %copy-start.15 = (s32[2,1]{0,1:T(1,128)S(1)}, s32[2,1]{0,1:T(1,128)}, u32[]{:S(2)}) copy-start(s32[2,1]{0,1:T(1,128)} %param.16) | copy-start | bytes 28
  10.0 23.8 %copy-start.14 = (s32[2]{0:T(128)S(1)}, s32[2]{0:T(128)}, u32[]{:S(2)}) copy-start(s32[2]{0:T(128)} %param.19) | copy-start | bytes 28
  10.0 119.1 %all-to-all-start = ((f32[128,2,16,128]{3,2,1,0:T(8,128)}), f32[128,2,16,128]{3,2,1,0:T(8,128)}, u32[]{:S(2)}, u32[]{:S(2)}) async-start(f32[128,2,16,128]{3,2,1,0:T(8,128)} %stack.43), calls=%async_computation | async-start | bytes 4194304 | tf_op jit(solution)/shard_map/all_to_all | solution.py:134
  30.7 100.6 %copy-start.1 = (f32[2,16,16,16]{3,2,1,0:T(8,128)S(1)}, f32[2,16,16,16]{3,2,1,0:T(8,128)}, u32[]{:S(2)}) copy-start(f32[2,16,16,16]{3,2,1,0:T(8,128)} %param.17) | copy-start | bytes 98308
  30.7 101.4 %copy-start.11 = (f32[2,16,256]{2,1,0:T(8,128)S(1)}, f32[2,16,256]{2,1,0:T(8,128)}, u32[]{:S(2)}) copy-start(f32[2,16,256]{2,1,0:T(8,128)} %param.21) | copy-start | bytes 98308
  30.7 156.1 %all-reduce.5.cloned.1.call-start = ((), (), s32[]{:S(2)}) async-start(), calls=%async_computation.4 | async-start | bytes 524288 | tf_op jit(solution)/shard_map/psum | solution.py:147
  30.7 3.1 collective-permute-start
  32.3 4.6 collective-permute-start.1
  131.3 56.6 %copy-start.10 = (f32[2,16,256]{2,1,0:T(8,128)S(1)}, f32[2,16,256]{2,1,0:T(8,128)}, u32[]{:S(2)}) copy-start(f32[2,16,256]{2,1,0:T(8,128)} %param.20) | copy-start | bytes 98308
  189.7 17.6 %copy-start.3 = (f32[512,128]{0,1:T(8,128)S(1)}, f32[512,128]{0,1:T(8,128)}, u32[]{:S(2)}) copy-start(f32[512,128]{0,1:T(8,128)} %all-reduce.5.cloned.1.call-done) | copy-start | bytes 786436
  189.7 116.0 %all-to-all-start.1 = ((f32[128,2,16,128]{3,2,1,0:T(8,128)}), f32[128,2,16,128]{3,2,1,0:T(8,128)}, u32[]{:S(2)}, u32[]{:S(2)}) async-start(f32[128,2,16,128]{3,2,1,0:T(8,128)} %stack.45), calls=%async_computation.1 | async-start | bytes 4194304 | tf_op jit(solution)/shard_map/all_to_all | solution.py:134
  207.2 156.3 %all-reduce.7.cloned.1.call-start = ((), (), s32[]{:S(2)}) async-start(), calls=%async_computation.5 | async-start | bytes 524288 | tf_op jit(solution)/shard_map/psum | solution.py:147
  207.3 2.8 collective-permute-start.2
  208.7 4.6 collective-permute-start.3
  366.5 17.6 %copy-start.4 = (f32[512,128]{0,1:T(8,128)S(1)}, f32[512,128]{0,1:T(8,128)}, u32[]{:S(2)}) copy-start(f32[512,128]{0,1:T(8,128)} %all-reduce.7.cloned.1.call-done) | copy-start | bytes 786436
  366.5 116.0 %all-to-all-start.2 = ((f32[128,2,16,128]{3,2,1,0:T(8,128)}), f32[128,2,16,128]{3,2,1,0:T(8,128)}, u32[]{:S(2)}, u32[]{:S(2)}) async-start(f32[128,2,16,128]{3,2,1,0:T(8,128)} %stack.47), calls=%async_computation.2 | async-start | bytes 4194304 | tf_op jit(solution)/shard_map/all_to_all | solution.py:134
  384.0 156.3 %all-reduce.9.cloned.1.call-start = ((), (), s32[]{:S(2)}) async-start(), calls=%async_computation.6 | async-start | bytes 524288 | tf_op jit(solution)/shard_map/psum | solution.py:147
  384.1 3.0 collective-permute-start.4
  385.5 4.6 collective-permute-start.5
  543.3 17.6 %copy-start.5 = (f32[512,128]{0,1:T(8,128)S(1)}, f32[512,128]{0,1:T(8,128)}, u32[]{:S(2)}) copy-start(f32[512,128]{0,1:T(8,128)} %all-reduce.9.cloned.1.call-done) | copy-start | bytes 786436
  543.3 116.0 %all-to-all-start.3 = ((f32[128,2,16,128]{3,2,1,0:T(8,128)}), f32[128,2,16,128]{3,2,1,0:T(8,128)}, u32[]{:S(2)}, u32[]{:S(2)}) async-start(f32[128,2,16,128]{3,2,1,0:T(8,128)} %stack.49), calls=%async_computation.3 | async-start | bytes 4194304 | tf_op jit(solution)/shard_map/all_to_all | solution.py:134
  560.8 156.3 %all-reduce.11.cloned.1.call-start = ((), (), s32[]{:S(2)}) async-start(), calls=%async_computation.7 | async-start | bytes 524288 | tf_op jit(solution)/shard_map/psum | solution.py:147
  560.8 2.8 collective-permute-start.6
  562.3 4.6 collective-permute-start.7
  662.2 3.9 copy-start.12
  666.1 51.1 %copy-start.9 = (f32[1,512,128]{1,0,2:T(1,128)S(1)}, f32[1,512,128]{1,0,2:T(1,128)}, u32[]{:S(2)}) copy-start(f32[1,512,128]{1,0,2:T(1,128)} %copy.52) | copy-start | bytes 786436
  725.3 502.8 %copy-start.6 = (f32[512,128]{0,1:T(8,128)S(1)}, f32[512,128]{0,1:T(8,128)}, u32[]{:S(2)}) copy-start(f32[512,128]{0,1:T(8,128)} %all-reduce.9.cloned.1.call-done) | copy-start | bytes 786436
  725.3 502.8 %copy-start.7 = (f32[512,128]{0,1:T(8,128)S(1)}, f32[512,128]{0,1:T(8,128)}, u32[]{:S(2)}) copy-start(f32[512,128]{0,1:T(8,128)} %copy.41) | copy-start | bytes 786436
  725.3 502.8 %copy-start.8 = (f32[512,128]{0,1:T(8,128)S(1)}, f32[512,128]{0,1:T(8,128)}, u32[]{:S(2)}) copy-start(f32[512,128]{0,1:T(8,128)} %copy.42) | copy-start | bytes 786436
  (1 other events, 0.6 us)
Sparse Core Ops, SparseCore 0:
  134.4 52.3 all-reduce.4
  310.9 52.5 all-reduce.6
  487.7 52.5 all-reduce.8
  664.5 52.5 all-reduce.10
